TPU v7x, 32 devices: a whole 2x2x4 slice. The times are simulated.
32 devices in a mesh: groups: 2 (over x), frame: 16 (over z, y, core).
Axes of the slice: x: 2, y: 2, z: 4, core: 2. Of those that a mesh axis runs over, the one named last changes fastest.
Arguments:
- video_qkv: bfloat16 [3, 32, 128, 1536], P(None, ('groups', 'frame')), parts along dimension 1, may hold values from -8 to 8
- text_qkv: bfloat16 [3, 512, 1536], P(None, ('groups', 'frame')), parts along dimension 1, may hold values from -8 to 8
- head_kind: int32 [24], P('groups'), parts along dimension 0, may hold values from 0 to 1, as said below
- text_len: int32 [2], P('groups'), parts along dimension 0, may hold values from 64 to 256
Outputs:
- video_out: bfloat16 [32, 128, 1536], P(('groups', 'frame')), parts along dimension 0
- text_out: bfloat16 [512, 1536], P(('groups', 'frame')), parts along dimension 0
There are 2 independent parts, one for each index of `groups`. A program takes and returns all parts, laid end to end along the dimension named above; each array names one. Nothing has to cross between parts.
Inputs may be any that keep to these rules, and one draw needn't show every extreme that they name: `head_kind`: exactly 6 of the 12 entries are 1.
All inputs are finite; a program needn't handle non-finite values.
Results may differ from a plain program's by a relative error of at most 0.009.
Values may be sent and summed in bfloat16 or wider, within the bound.
A program may use at most 448 MiB of HBM per device.

v0:
```python
import jax
import jax.numpy as jnp
from jax import lax
from jax.sharding import PartitionSpec as P

masked_score = -1e30


def body(video_qkv, text_qkv, head_kind, text_len):
    head_count = head_kind.shape[0]
    head_width = video_qkv.shape[-1]
    head_dim = head_width // head_count
    positions = video_qkv.shape[2]
    shard_text = text_qkv.shape[1]
    score_scale = head_dim ** (-0.5)
    device_rank = lax.axis_index("frame")
    local_video = video_qkv.reshape(3, 1, positions, head_count, head_dim)
    gathered = lax.all_gather(text_qkv, "frame", axis=1, tiled=True)
    text_total = gathered.shape[1]
    all_text = gathered.reshape(3, text_total, head_count, head_dim)
    text_valid = jnp.arange(text_total) < text_len[0]
    spatial_heads = jnp.nonzero(head_kind == 0, size=head_count - head_count // 2)[0].astype(
        jnp.int32
    )
    temporal_heads = jnp.nonzero(head_kind == 1, size=head_count // 2)[0].astype(jnp.int32)
    own_frame = jnp.take(local_video[:, 0], spatial_heads, axis=2)
    text_spatial = jnp.take(all_text[1:], spatial_heads, axis=2)
    joint_keys = jnp.concatenate([own_frame[1], text_spatial[0]], axis=0)
    joint_values = jnp.concatenate([own_frame[2], text_spatial[1]], axis=0)
    joint_valid = jnp.concatenate([jnp.ones((positions,), bool), text_valid])
    spatial_scores = (
        jnp.einsum("phd,khd->hpk", own_frame[0], joint_keys, preferred_element_type=jnp.float32)
        * score_scale
    )
    spatial_scores = jnp.where(joint_valid, spatial_scores, masked_score)
    row_max = spatial_scores.max(-1, keepdims=True)
    spatial_exp = jnp.exp(spatial_scores - row_max)
    totals = spatial_exp.sum(-1)
    summed = jnp.einsum(
        "hpk,khd->phd",
        spatial_exp.astype(jnp.bfloat16),
        joint_values,
        preferred_element_type=jnp.float32,
    )
    spatial_result = (summed / totals.T[..., None]).astype(jnp.bfloat16)
    selected = jnp.take(local_video, temporal_heads, axis=3)
    block = lax.all_to_all(selected, "frame", split_axis=2, concat_axis=1, tiled=True)
    scores = (
        jnp.einsum("fphd,gphd->phfg", block[0], block[1], preferred_element_type=jnp.float32)
        * score_scale
    )
    block_max = scores.max(-1, keepdims=True)
    exps = jnp.exp(scores - block_max)
    block_totals = exps.sum(-1)
    block_sum = jnp.einsum(
        "phfg,gphd->fphd", exps.astype(jnp.bfloat16), block[2], preferred_element_type=jnp.float32
    )
    result = (block_sum / jnp.transpose(block_totals, (2, 0, 1))[..., None]).astype(jnp.bfloat16)
    temporal_result = lax.all_to_all(result, "frame", split_axis=0, concat_axis=1, tiled=True)[0]
    joined = jnp.concatenate([spatial_result, temporal_result], axis=1)
    order = jnp.concatenate([spatial_heads, temporal_heads])
    inverse = jnp.argsort(order)
    video_out = jnp.take(joined, inverse, axis=1).reshape(1, positions, head_width)
    text_queries = all_text[0]
    own_text = text_qkv.reshape(3, shard_text, head_count, head_dim)
    own_valid = device_rank * shard_text + jnp.arange(shard_text) < text_len[0]
    local_keys = jnp.concatenate([local_video[1, 0], own_text[1]], axis=0)
    local_values = jnp.concatenate([local_video[2, 0], own_text[2]], axis=0)
    local_valid = jnp.concatenate([jnp.ones((positions,), bool), own_valid])
    query_scores = (
        jnp.einsum("thd,khd->thk", text_queries, local_keys, preferred_element_type=jnp.float32)
        * score_scale
    )
    query_scores = jnp.where(local_valid, query_scores, masked_score)
    local_max = query_scores.max(-1)
    global_max = lax.pmax(local_max, "frame")
    query_exp = jnp.exp(query_scores - global_max[..., None])
    query_totals = query_exp.sum(-1)
    query_sums = jnp.einsum(
        "thk,khd->thd",
        query_exp.astype(jnp.bfloat16),
        local_values,
        preferred_element_type=jnp.float32,
    )
    query_totals, query_sums = (query_totals, query_sums)
    query_sums, query_totals = (
        lax.psum_scatter(query_sums, "frame", scatter_dimension=0, tiled=True),
        lax.psum_scatter(query_totals, "frame", scatter_dimension=0, tiled=True),
    )
    text_out = (
        (query_sums / query_totals[..., None]).astype(jnp.bfloat16).reshape(shard_text, head_width)
    )
    return (video_out, text_out)


def solution(mesh):
    in_specs = (
        P(None, ("groups", "frame"), None, None),
        P(None, ("groups", "frame"), None),
        P("groups"),
        P("groups"),
    )
    out_specs = (P(("groups", "frame"), None, None), P(("groups", "frame"), None))
    return jax.shard_map(body, mesh=mesh, in_specs=in_specs, out_specs=out_specs, check_vma=False)
```

profile of v0, /device:TPU:0, one launch (start us, length us, event | category | flops | bytes accessed | tf_op | source)
XLA Modules:
  0.0 248.0 jit_solution(8122713932160356328)
XLA Ops:
  7.2 0.7 all-gather.2.cloned.1.call-update
  7.9 0.7 fusion.43
  8.9 0.6 scatter_custom_fusion
  9.6 0.6 scatter_custom_fusion.1
  10.6 1.7 copy.94
  12.3 0.7 copy.95
  13.0 0.6 fusion.44
  13.7 1.3 fusion.41
  15.0 0.7 gather_fusion.2
  15.7 1.8 compare_and_fusion
  17.7 1.4 copy.102
  19.1 7.4 %all-to-all-start = ((bf16[3,1,128,6,128]{4,0,3,1,2:T(4,128)(2,1)}), bf16[3,1,128,6,128]{4,0,3,1,2:T(4,128)(2,1)S(1)}, u32[]{:S(2)}, u32[]{:S(2)}) async-start(bf16[3,1,128,6,128]{4,0,3,1,2:T(4,128)(2,1)} %copy.102), calls=%async_computation | async-start | bytes 1572864 | tf_op jit(solution)/shard_map/all_to_all | solution.py:47
  27.2 0.6 copy.116
  27.9 0.6 copy.119
  28.6 0.8 fusion.57
  29.4 1.2 copy.133
  30.6 0.9 copy.115
  32.0 0.7 gather_fusion
  32.8 1.2 sort.17
  34.1 0.9 fusion.23
  35.1 11.1 %all-to-all-done = bf16[3,1,128,6,128]{4,0,3,1,2:T(4,128)(2,1)S(1)} async-done(((bf16[3,1,128,6,128]{4,0,3,1,2:T(4,128)(2,1)}), bf16[3,1,128,6,128]{4,0,3,1,2:T(4,128)(2,1)S(1)}, u32[]{:S(2)}, u32[]{:S(2)}) %all-to-all-start) | async-done | bytes 589856 | tf_op jit(solution)/shard_map/all_to_all | solution.py:47
  46.1 0.8 fusion.58
  47.0 0.7 copy.160
  48.1 0.7 copy-done.2
  48.9 11.8 %all-gather.2.cloned.1.call-done = bf16[3,256,1536]{2,1,0:T(8,128)(2,1)} async-done(((bf16[3,16,1536]{2,1,0:T(8,128)(2,1)}), bf16[3,256,1536]{2,1,0:T(8,128)(2,1)}) %all-gather.2.cloned.1.call-update) | async-done | bytes 2359312 | tf_op jit(solution)/shard_map/all_gather | solution.py:18
  60.7 1.1 slice-done
  62.6 59.1 %pmax.7 = f32[256,12]{0,1:T(8,128)S(1)} all-reduce(f32[256,12]{0,1:T(8,128)S(1)} %get-tuple-element.31), channel_id=1, replica_groups=mesh['groups'=2,'frame'=16] {'frame'}, use_global_device_ids=true, to_apply=%region_14.15 | all-reduce | flops 3072 | bytes 24576 | tf_op jit(solution)/shard_map/pmax | solution.py:76
  122.2 0.8 copy.127
  123.0 1.7 convolution_bitcast_fusion
  124.7 1.9 copy.122
  126.7 1.0 copy-done.3
  128.0 0.8 copy.110
  128.7 3.5 %all-to-all-start.1 = ((bf16[16,8,6,128]{3,1,2,0:T(8,128)(2,1)}), bf16[16,8,6,128]{3,1,2,0:T(8,128)(2,1)S(1)}, u32[]{:S(2)}, u32[]{:S(2)}) async-start(bf16[16,8,6,128]{3,1,2,0:T(8,128)(2,1)} %copy.110), calls=%async_computation.1 | async-start | bytes 393216 | tf_op jit(solution)/shard_map/all_to_all | solution.py:59
  132.8 0.7 slice_bitcast_fusion.5
  133.5 7.7 %all-to-all-done.1 = bf16[16,8,6,128]{3,1,2,0:T(8,128)(2,1)S(1)} async-done(((bf16[16,8,6,128]{3,1,2,0:T(8,128)(2,1)}), bf16[16,8,6,128]{3,1,2,0:T(8,128)(2,1)S(1)}, u32[]{:S(2)}, u32[]{:S(2)}) %all-to-all-start.1) | async-done | bytes 196640 | tf_op jit(solution)/shard_map/all_to_all | solution.py:59
  141.4 1.4 slice-done.1
  142.8 0.7 copy.129
  143.5 0.9 copy.98
  144.4 0.7 gather_fusion.1
  145.4 0.7 copy-done.7
  146.1 1.4 fusion.61
  147.9 0.5 fusion.6
  148.5 0.6 gather_fusion.3
  149.3 0.8 broadcast_select_fusion
  150.1 25.4 %reduce-scatter.7.cloned.1.call-done = f32[16,12]{1,0:T(8,128)} async-done(((f32[256,12]{1,0:T(8,128)}), f32[16,12]{1,0:T(8,128)}) %reduce-scatter.7.cloned.1.call-update) | async-done | bytes 784 | tf_op jit(solution)/shard_map/reduce_scatter | solution.py:88
  175.4 64.4 %reduce-scatter.5.cloned.1.call-done = f32[16,12,128]{2,1,0:T(8,128)} async-done(((f32[256,12,128]{2,1,0:T(8,128)}), f32[16,12,128]{2,1,0:T(8,128)}) %reduce-scatter.5.cloned.1.call-update) | async-done | bytes 98320 | tf_op jit(solution)/shard_map/reduce_scatter | solution.py:87
  239.8 1.0 divide_convert_fusion
  240.8 0.6 copy.162
  (70 shorter events, 5.3 us)
Async XLA Ops:
  7.2 53.6 %all-gather.2.cloned.1.call-start = ((), (), s32[]{:S(2)}) async-start(), calls=%async_computation.4 | async-start | bytes 2506752 | tf_op jit(solution)/shard_map/all_gather | solution.py:18
  12.3 0.8 copy-start.11
  17.6 9.5 %copy-start.4 = (bf16[3,16,1536]{2,1,0:T(8,128)(2,1)S(1)}, bf16[3,16,1536]{2,1,0:T(8,128)(2,1)}, u32[]{:S(2)}) copy-start(bf16[3,16,1536]{2,1,0:T(8,128)(2,1)} %param.5) | copy-start | bytes 442372
  17.6 10.9 %copy-start = (bf16[3,1,128,1536]{3,2,1,0:T(8,128)(2,1)S(1)}, bf16[3,1,128,1536]{3,2,1,0:T(8,128)(2,1)}, u32[]{:S(2)}) copy-start(bf16[3,1,128,1536]{3,2,1,0:T(8,128)(2,1)} %param.4) | copy-start | bytes 3538948
  19.1 27.1 %all-to-all-start = ((bf16[3,1,128,6,128]{4,0,3,1,2:T(4,128)(2,1)}), bf16[3,1,128,6,128]{4,0,3,1,2:T(4,128)(2,1)S(1)}, u32[]{:S(2)}, u32[]{:S(2)}) async-start(bf16[3,1,128,6,128]{4,0,3,1,2:T(4,128)(2,1)} %copy.102), calls=%async_computation | async-start | bytes 1572864 | tf_op jit(solution)/shard_map/all_to_all | solution.py:47
  26.4 149.0 %reduce-scatter.7.cloned.1.call-start = ((), (), s32[]{:S(2)}) async-start(), calls=%async_computation.6 | async-start | bytes 139264 | tf_op jit(solution)/shard_map/reduce_scatter | solution.py:88
  31.5 1.2 copy-start.9
  31.5 1.2 copy-start.10
  48.0 0.7 copy-start.2
  48.9 13.2 %copy-start.8 = (bf16[16,12,128]{2,0,1:T(8,128)(2,1)S(1)}, bf16[16,12,128]{2,0,1:T(8,128)(2,1)}, u32[]{:S(2)}) copy-start(bf16[16,12,128]{2,0,1:T(8,128)(2,1)} %copy.119) | copy-start | bytes 147460
  60.7 1.1 slice-start
  62.6 60.4 %copy-start.5 = (bf16[16,12,128]{2,0,1:T(8,128)(2,1)S(1)}, bf16[16,12,128]{2,0,1:T(8,128)(2,1)}, u32[]{:S(2)}) copy-start(bf16[16,12,128]{2,0,1:T(8,128)(2,1)} %copy.116) | copy-start | bytes 147460
  122.9 116.9 %reduce-scatter.5.cloned.1.call-start = ((), (), s32[]{:S(2)}) async-start(), calls=%async_computation.5 | async-start | bytes 2228224 | tf_op jit(solution)/shard_map/reduce_scatter | solution.py:87
  126.6 1.0 copy-start.3
  126.6 1.0 copy-start.6
  126.6 6.1 %copy-start.1 = (bf16[3,128,6,128]{3,1,2,0:T(8,128)(2,1)S(1)}, bf16[3,128,6,128]{3,1,2,0:T(8,128)(2,1)}, u32[]{:S(2)}) copy-start(bf16[3,128,6,128]{3,1,2,0:T(8,128)(2,1)} %fusion.23) | copy-start | bytes 1769476
  128.7 12.5 %all-to-all-start.1 = ((bf16[16,8,6,128]{3,1,2,0:T(8,128)(2,1)}), bf16[16,8,6,128]{3,1,2,0:T(8,128)(2,1)S(1)}, u32[]{:S(2)}, u32[]{:S(2)}) async-start(bf16[16,8,6,128]{3,1,2,0:T(8,128)(2,1)} %copy.110), calls=%async_computation.1 | async-start | bytes 393216 | tf_op jit(solution)/shard_map/all_to_all | solution.py:59
  141.4 1.4 slice-start.1
  145.1 0.9 copy-start.7
  145.2 0.9 copy-start.12
Sparse Core Ops, SparseCore 0:
  10.3 50.3 all-gather.1
  123.1 52.3 reduce-scatter.6
  179.2 60.5 reduce-scatter.4
where the time goes:
time: 249 us; the launch traced here: 248 us
  waiting for transfers between devices  121 us (49%)
  blocking collectives  59.1 us (24%)
  local copies, waits for them, and re-layouts  25.6 us (10%)
  between operations  14.8 us (6%)
  other arithmetic  11.8 us (5%)
  starting transfers between devices  11 us (4%)
  matrix products  4.6 us (2%)
    reduce_scatter x1, waiting for transfers between devices, body(): lax.psum_scatter(query_sums, 'frame', scatter_dimension=0, tiled=True)  64.4 us
    pmax x1, blocking collectives, body(): global_max = lax.pmax(local_max, 'frame')  59.1 us
    reduce_scatter x1, waiting for transfers between devices, body(): lax.psum_scatter(query_totals, 'frame', scatter_dimension=0, tiled=True)  25.4 us
    all_gather x1, waiting for transfers between devices, body(): gathered = lax.all_gather(text_qkv, 'frame', axis=1, tiled=True)  11.8 us
    all_to_all x1, waiting for transfers between devices, body(): lax.all_to_all(selected, 'frame', split_axis=2, concat_axis=1, tiled=True)  11.1 us
    unnamed x36, local copies, waits for them, and re-layouts  8.76 us
    all_to_all x1, waiting for transfers between devices, body(): lax.all_to_all(result, 'frame', split_axis=0, concat_axis=1, tiled=True)[0]  7.7 us
    all_to_all x1, starting transfers between devices, body(): lax.all_to_all(selected, 'frame', split_axis=2, concat_axis=1, tiled=True)  7.39 us
  transfers between devices with their start and end apart: 5, of which 5 were waited for; matrix products, arithmetic and copies ran while one was open for 13% of the time, Pallas kernels for 0%

commit v1 on v0

--- a/solution.py
+++ b/solution.py
@@ -1,12 +1,16 @@
+import functools
+
 import jax
 import jax.numpy as jnp
 from jax import lax
+from jax.experimental import pallas as pl
+from jax.experimental.pallas import tpu as pltpu
 from jax.sharding import PartitionSpec as P
 
 masked_score = -1e30
 
 
-def body(video_qkv, text_qkv, head_kind, text_len):
+def plain_body(video_qkv, text_qkv, head_kind, text_len):
     head_count = head_kind.shape[0]
     head_width = video_qkv.shape[-1]
     head_dim = head_width // head_count
@@ -93,6 +97,426 @@
     return (video_out, text_out)
 
 
+f32 = jnp.float32
+bf16 = jnp.bfloat16
+
+
+def dot_nt(a, b):
+    return lax.dot_general(a, b, (((1,), (1,)), ((), ())), preferred_element_type=f32)
+
+
+def dot_nn(a, b):
+    return lax.dot_general(a, b, (((1,), (0,)), ((), ())), preferred_element_type=f32)
+
+
+def softmax_parts(scores):
+    top = scores.max(-1, keepdims=True)
+    e = jnp.exp(scores - top)
+    return top, e.sum(-1, keepdims=True), e.astype(bf16)
+
+
+def remote(src, dst, send_sem, recv_sem, peer):
+    return pltpu.make_async_remote_copy(
+        src_ref=src,
+        dst_ref=dst,
+        send_sem=send_sem,
+        recv_sem=recv_sem,
+        device_id={"frame": peer},
+        device_id_type=pl.DeviceIdType.MESH,
+    )
+
+
+def kernel(
+    n,
+    heads,
+    kind_ref,
+    len_ref,
+    video_ref,
+    text_ref,
+    video_out,
+    text_out,
+    pair_video,
+    pair_text,
+    q_all,
+    kv_all,
+    t_send,
+    t_recv,
+    o_send,
+    o_recv,
+    p_send,
+    p_recv,
+    m_send,
+    m_recv,
+    result,
+    pair_s,
+    pair_r,
+    q_s,
+    q_r,
+    kv_s,
+    kv_r,
+    fw_s,
+    t_s,
+    t_r,
+    o_s,
+    o_r,
+    p_s,
+    p_r,
+    m_s,
+    m_r,
+):
+    half = heads // 2
+    twins = n // 2
+    positions = video_ref.shape[1]
+    hd = video_ref.shape[2] // heads
+    shard = text_ref.shape[1]
+    piece = positions // n
+    text_total = n * shard
+    rows = twins * shard
+    scale = hd ** (-0.5)
+    me = lax.axis_index("frame")
+    parity = lax.rem(me, 2)
+    partner = me + 1 - 2 * parity
+    mine = me // 2
+
+    barrier = pltpu.get_barrier_semaphore()
+
+    def greet(k, c):
+        pl.semaphore_signal(
+            barrier,
+            inc=1,
+            device_id={"frame": lax.rem(me + k, n)},
+            device_id_type=pl.DeviceIdType.MESH,
+        )
+        return c
+
+    lax.fori_loop(1, n, greet, 0)
+
+    spatial_seen = jnp.int32(0)
+    temporal_seen = jnp.int32(0)
+    places = []
+    for h in range(heads):
+        kind = kind_ref[h]
+        place = jnp.where(kind == 0, spatial_seen, half + temporal_seen)
+        places.append(place)
+        spatial_seen = spatial_seen + jnp.where(kind == 0, 1, 0)
+        temporal_seen = temporal_seen + jnp.where(kind == 0, 0, 1)
+
+    def in_slot(i, load):
+        first = i % half
+        block = load(slice(first * hd, (first + 1) * hd))
+        for h in range(first + 1, first + half + 1):
+            block = jnp.where(places[h] == i, load(slice(h * hd, (h + 1) * hd)), block)
+        return block
+
+    for i in range(half):
+        for t in range(2):
+            kv_all[me, t, :, i * hd : (i + 1) * hd] = in_slot(i, lambda c: text_ref[t + 1, :, c])
+    q_all[mine] = text_ref[0]
+
+    for i in range(half):
+        for t in range(3):
+            whole = in_slot(half + i, lambda c: video_ref[t, :, c])
+            whole = whole.astype(f32).reshape(n, piece, hd)
+            t_send[:, t, :, i * hd : (i + 1) * hd] = whole.astype(bf16)
+
+    pl.semaphore_wait(barrier, n - 1)
+
+    def pair_copies():
+        return (
+            remote(video_ref.at[1:3], pair_video, pair_s.at[0], pair_r.at[0], partner),
+            remote(text_ref.at[1:3], pair_text, pair_s.at[1], pair_r.at[1], partner),
+            remote(kv_all.at[me], kv_all.at[me], fw_s.at[mine], kv_r.at[me], partner),
+        )
+
+    for c in pair_copies():
+        c.start()
+
+    def twin(k):
+        return lax.rem(me + 2 * k, n)
+
+    def q_copy(to):
+        return remote(q_all.at[mine], q_all.at[mine], q_s.at[to // 2], q_r.at[mine], to)
+
+    def kv_copy(to):
+        return remote(kv_all.at[me], kv_all.at[me], kv_s.at[to // 2], kv_r.at[me], to)
+
+    def t_copy(to):
+        return remote(t_send.at[to], t_recv.at[me], t_s.at[to], t_r.at[me], to)
+
+    def landed(dst, sem):
+        remote(dst, dst, sem, sem, partner).wait_recv()
+
+    def sent(src, sem):
+        remote(src, src, sem, sem, partner).wait_send()
+
+    def start_q(k, c):
+        q_copy(twin(k)).start()
+        return c
+
+    def start_kv(k, c):
+        kv_copy(twin(k)).start()
+        return c
+
+    def start_t(k, c):
+        t_copy(lax.rem(me + k, n)).start()
+        return c
+
+    lax.fori_loop(1, twins, start_q, 0)
+    lax.fori_loop(1, n, start_t, 0)
+    lax.fori_loop(1, twins, start_kv, 0)
+    t_recv[me] = t_send[me]
+
+    landed(pair_video, pair_r.at[0])
+    landed(pair_text, pair_r.at[1])
+
+    def wait_q(k, c):
+        j = twin(k) // 2
+        landed(q_all.at[j], q_r.at[j])
+        return c
+
+    lax.fori_loop(1, twins, wait_q, 0)
+
+    length = len_ref[0]
+    key = lax.broadcasted_iota(jnp.int32, (1, 2 * positions + 2 * shard), 1)
+    offset = key - 2 * positions
+    token = jnp.where(offset < shard, me * shard + offset, partner * shard + offset - shard)
+    key_ok = (offset < 0) | (token < length)
+    lane = lax.broadcasted_iota(jnp.int32, (rows, 128), 1)
+    stats = jnp.where(lane < 64, 0.0, 1.0).astype(f32)
+    for h in range(heads):
+        hs = slice(h * hd, (h + 1) * hd)
+        q = q_all[:, :, hs].reshape(rows, hd)
+        keys = jnp.concatenate(
+            [video_ref[1, :, hs], pair_video[0, :, hs], text_ref[1, :, hs], pair_text[0, :, hs]],
+            axis=0,
+        )
+        values = jnp.concatenate(
+            [video_ref[2, :, hs], pair_video[1, :, hs], text_ref[2, :, hs], pair_text[1, :, hs]],
+            axis=0,
+        )
+        s = jnp.where(key_ok, dot_nt(q, keys) * scale, masked_score)
+        top, total, w = softmax_parts(s)
+        p_send[:, :, hs] = dot_nn(w, values).astype(bf16).reshape(twins, shard, hd)
+        stats = jnp.where(lane == h, top, jnp.where(lane == h + 64, total, stats))
+    m_send[...] = stats.reshape(twins, shard, 128)
+
+    def p_copy(to):
+        return remote(
+            p_send.at[to // 2], p_recv.at[mine], p_s.at[to // 2], p_r.at[mine], to
+        )
+
+    def m_copy(to):
+        return remote(
+            m_send.at[to // 2], m_recv.at[mine], m_s.at[to // 2], m_r.at[mine], to
+        )
+
+    def start_p(k, c):
+        p_copy(twin(k)).start()
+        m_copy(twin(k)).start()
+        return c
+
+    lax.fori_loop(1, twins, start_p, 0)
+    p_recv[mine] = p_send[mine]
+    m_recv[mine] = m_send[mine]
+
+    def wait_t(k, c):
+        j = lax.rem(me + k, n)
+        landed(t_recv.at[j], t_r.at[j])
+        return c
+
+    lax.fori_loop(1, n, wait_t, 0)
+    count = n * piece
+    row_at = lax.rem(lax.broadcasted_iota(jnp.int32, (count, count), 0), piece)
+    col_at = lax.rem(lax.broadcasted_iota(jnp.int32, (count, count), 1), piece)
+    same = row_at == col_at
+    for i in range(half):
+        hs = slice(i * hd, (i + 1) * hd)
+        q, k_, v = (
+            t_recv[:, t, :, hs].astype(f32).reshape(count, hd).astype(bf16) for t in range(3)
+        )
+        s = jnp.where(same, dot_nt(q, k_) * scale, masked_score)
+        top, total, w = softmax_parts(s)
+        o = dot_nn(w, v) / total
+        o_send[:, :, hs] = o.reshape(n, piece, hd).astype(bf16)
+
+    def o_copy(to):
+        return remote(o_send.at[to], o_recv.at[me], o_s.at[to], o_r.at[me], to)
+
+    def start_o(k, c):
+        o_copy(lax.rem(me + k, n)).start()
+        return c
+
+    lax.fori_loop(1, n, start_o, 0)
+    o_recv[me] = o_send[me]
+
+    def fw_copy(j):
+        return remote(kv_all.at[j], kv_all.at[j], fw_s.at[j // 2], kv_r.at[j], partner)
+
+    def forward(k, c):
+        j = lax.rem(me + n - 2 * k, n)
+        landed(kv_all.at[j], kv_r.at[j])
+        fw_copy(j).start()
+        return c
+
+    lax.fori_loop(1, twins, forward, 0)
+
+    def wait_kv(k, c):
+        j = lax.rem(partner + 2 * k, n)
+        landed(kv_all.at[j], kv_r.at[j])
+        return c
+
+    lax.fori_loop(0, twins, wait_kv, 0)
+    text_key = lax.broadcasted_iota(jnp.int32, (1, positions + text_total), 1) - positions
+    joint_ok = text_key < length
+    for i in range(half):
+        q, k_, v = (in_slot(i, lambda c: video_ref[t, :, c]) for t in range(3))
+        hs = slice(i * hd, (i + 1) * hd)
+        keys = jnp.concatenate(
+            [k_, kv_all[:, 0, :, hs].reshape(text_total, hd)], axis=0
+        )
+        values = jnp.concatenate(
+            [v, kv_all[:, 1, :, hs].reshape(text_total, hd)], axis=0
+        )
+        s = jnp.where(joint_ok, dot_nt(q, keys) * scale, masked_score)
+        top, total, w = softmax_parts(s)
+        result[i] = (dot_nn(w, values) / total).astype(bf16)
+
+    for h in range(heads):
+        block = result[max(0, h - half)]
+        for i in range(max(0, h - half) + 1, min(h, half - 1) + 1):
+            block = jnp.where(places[h] == i, result[i], block)
+        video_out[:, h * hd : (h + 1) * hd] = block
+
+    def wait_p(k, c):
+        j = twin(k) // 2
+        landed(p_recv.at[j], p_r.at[j])
+        landed(m_recv.at[j], m_r.at[j])
+        return c
+
+    lax.fori_loop(1, twins, wait_p, 0)
+    tops = m_recv[...]
+    sums = pltpu.roll(tops.reshape(rows, 128), 64, 1).reshape(twins, shard, 128)
+    best = tops.max(0, keepdims=True)
+    weight = jnp.exp(jnp.minimum(tops - best, 0.0))
+    total = (weight * sums).sum(0)
+    for h in range(heads):
+        hs = slice(h * hd, (h + 1) * hd)
+        merged = (weight[:, :, h : h + 1] * p_recv[:, :, hs].astype(f32)).sum(0)
+        text_out[:, hs] = (merged / total[:, h : h + 1]).astype(bf16)
+
+    def wait_o(k, c):
+        j = lax.rem(me + k, n)
+        landed(o_recv.at[j], o_r.at[j])
+        return c
+
+    lax.fori_loop(1, n, wait_o, 0)
+    for i in range(half):
+        hs = slice(i * hd, (i + 1) * hd)
+        result[half + i] = o_recv[:, :, hs].astype(f32).reshape(positions, hd).astype(bf16)
+    for h in range(heads):
+        hs = slice(h * hd, (h + 1) * hd)
+        block = video_out[:, hs]
+        for i in range(max(0, h - half), min(h, half - 1) + 1):
+            block = jnp.where(places[h] == half + i, result[half + i], block)
+        video_out[:, hs] = block
+
+    sent(pair_video, pair_s.at[0])
+    sent(pair_text, pair_s.at[1])
+    sent(kv_all.at[me], fw_s.at[mine])
+
+    def drain_twin(k, c):
+        j = twin(k) // 2
+        sent(q_all.at[j], q_s.at[j])
+        sent(kv_all.at[me], kv_s.at[j])
+        sent(kv_all.at[me], fw_s.at[j])
+        sent(p_send.at[j], p_s.at[j])
+        sent(m_send.at[j], m_s.at[j])
+        return c
+
+    lax.fori_loop(1, twins, drain_twin, 0)
+
+    def drain_all(k, c):
+        j = lax.rem(me + k, n)
+        sent(t_send.at[j], t_s.at[j])
+        sent(o_send.at[j], o_s.at[j])
+        return c
+
+    lax.fori_loop(1, n, drain_all, 0)
+
+
+def fused_body(n, video_qkv, text_qkv, head_kind, text_len):
+    heads = head_kind.shape[0]
+    _, _, positions, width = video_qkv.shape
+    shard = text_qkv.shape[1]
+    half, twins, piece = heads // 2, n // 2, positions // n
+    hd = width // heads
+    narrow = half * hd
+    vmem = pl.BlockSpec(memory_space=pltpu.VMEM)
+    smem = pl.BlockSpec(memory_space=pltpu.SMEM)
+    dma = pltpu.SemaphoreType.DMA
+    video_out, text_out = pl.pallas_call(
+        functools.partial(kernel, n, heads),
+        out_shape=(
+            jax.ShapeDtypeStruct((positions, width), bf16),
+            jax.ShapeDtypeStruct((shard, width), bf16),
+        ),
+        in_specs=[smem, smem, vmem, vmem],
+        out_specs=(vmem, vmem),
+        scratch_shapes=[
+            pltpu.VMEM((2, positions, width), bf16),
+            pltpu.VMEM((2, shard, width), bf16),
+            pltpu.VMEM((twins, shard, width), bf16),
+            pltpu.VMEM((n, 2, shard, narrow), bf16),
+            pltpu.VMEM((n, 3, piece, narrow), bf16),
+            pltpu.VMEM((n, 3, piece, narrow), bf16),
+            pltpu.VMEM((n, piece, narrow), bf16),
+            pltpu.VMEM((n, piece, narrow), bf16),
+            pltpu.VMEM((twins, shard, width), bf16),
+            pltpu.VMEM((twins, shard, width), bf16),
+            pltpu.VMEM((twins, shard, 128), f32),
+            pltpu.VMEM((twins, shard, 128), f32),
+            pltpu.VMEM((heads, positions, hd), bf16),
+            dma((2,)),
+            dma((2,)),
+            dma((twins,)),
+            dma((twins,)),
+            dma((twins,)),
+            dma((n,)),
+            dma((twins,)),
+            dma((n,)),
+            dma((n,)),
+            dma((n,)),
+            dma((n,)),
+            dma((twins,)),
+            dma((twins,)),
+            dma((twins,)),
+            dma((twins,)),
+        ],
+        compiler_params=pltpu.CompilerParams(
+            collective_id=0, has_side_effects=True, vmem_limit_bytes=40 << 20
+        ),
+    )(head_kind, text_len, video_qkv.reshape(3, positions, width), text_qkv)
+    return video_out.reshape(1, positions, width), text_out
+
+
+def body(n, video_qkv, text_qkv, head_kind, text_len):
+    heads = head_kind.shape[0]
+    positions, width = video_qkv.shape[2:]
+    shard = text_qkv.shape[1]
+    whole_tiles = (
+        video_qkv.shape[1] == 1
+        and n % 2 == 0
+        and heads % 2 == 0
+        and heads <= 64
+        and shard % 16 == 0
+        and positions % (8 * n) == 0
+        and (width // heads) % 128 == 0
+    )
+    if whole_tiles:
+        return fused_body(n, video_qkv, text_qkv, head_kind, text_len)
+    return plain_body(video_qkv, text_qkv, head_kind, text_len)
+
+
 def solution(mesh):
     in_specs = (
         P(None, ("groups", "frame"), None, None),
@@ -101,4 +525,5 @@
         P("groups"),
     )
     out_specs = (P(("groups", "frame"), None, None), P(("groups", "frame"), None))
-    return jax.shard_map(body, mesh=mesh, in_specs=in_specs, out_specs=out_specs, check_vma=False)
+    return jax.shard_map(
+        functools.partial(body, mesh.shape["frame"]), mesh=mesh, in_specs=in_specs, out_specs=out_specs, check_vma=False)

time: 249 us -> 57.9 us (0.23)
  waiting for transfers between devices: 121 us -> 0 us
  blocking collectives: 59.1 us -> 0 us
  Pallas kernels: 0 us -> 52.2 us
  local copies, waits for them, and re-layouts: 25.6 us -> 4.2 us
  between operations: 14.8 us -> 1.3 us
  other arithmetic: 11.8 us -> 0 us
  starting transfers between devices: 11 us -> 0 us
  matrix products: 4.6 us -> 0 us
    reduce_scatter x2 -> x0, waiting for transfers between devices: 89.7 us -> none  [the longest x1 64.4 us: body(): lax.psum_scatter(query_sums, 'frame', scatter_dimension=0, tiled=True)]
    pmax x1 -> x0, blocking collectives: 59.1 us -> none  [body(): global_max = lax.pmax(local_max, 'frame')]
    pallas_call x0 -> x1, Pallas kernels: none -> 52.2 us  [fused_body(): pl.pallas_call(functools.partial(kernel, n, heads), out_shape=(jax.ShapeD...]
    all_to_all x2 -> x0, waiting for transfers between devices: 18.8 us -> none  [the longest x1 11.1 us: body(): lax.all_to_all(selected, 'frame', split_axis=2, concat_axis=1, tiled=True)]
    all_gather x1 -> x0, waiting for transfers between devices: 11.8 us -> none  [body(): gathered = lax.all_gather(text_qkv, 'frame', axis=1, tiled=True)]
    all_to_all x2 -> x0, starting transfers between devices: 10.9 us -> none  [the longest x1 7.39 us: body(): lax.all_to_all(selected, 'frame', split_axis=2, concat_axis=1, tiled=True)]
    slice x8 -> x0, local copies, waits for them, and re-layouts: 5.08 us -> none  [the longest x3 2.31 us: body(): text_spatial = jnp.take(all_text[1:], spatial_heads, axis=2)]
    dot_general x6 -> x0, matrix products: 4.6 us -> none  [the longest x1 1.69 us: body(): jnp.einsum('thk,khd->thd', query_exp.astype(jnp.bfloat16), local_values,...]
  transfers between devices with their start and end apart: 5 -> 0, of which waited for: 5 -> 0; matrix products, arithmetic and copies ran while one was open for 13% -> 0% of each run, Pallas kernels for 0% -> 0%
where the time goes in v1:
time: 57.9 us; the launch traced here: 57.7 us
  Pallas kernels  52.2 us (90%)
  local copies, waits for them, and re-layouts  4.2 us (7%)
  between operations  1.3 us (2%)
    pallas_call x1, Pallas kernels, fused_body(): pl.pallas_call(functools.partial(kernel, n, heads), out_shape=(jax.ShapeD...  52.2 us
    unnamed x8, local copies, waits for them, and re-layouts  4.2 us

profile of v1, /device:TPU:0, one launch (start us, length us, event | category | flops | bytes accessed | tf_op | source)
XLA Modules:
  0.0 57.7 jit_solution(6442149254963570630)
XLA Ops:
  1.3 0.0 copy-start
  1.3 1.3 %copy-done = bf16[3,1,128,1536]{3,2,1,0:T(8,128)(2,1)S(1)} copy-done((bf16[3,1,128,1536]{3,2,1,0:T(8,128)(2,1)S(1)}, bf16[3,1,128,1536]{3,2,1,0:T(8,128)(2,1)}, u32[]{:S(2)}) %copy-start) | copy-done | bytes 1179672
  2.5 0.0 copy-start.1
  2.6 0.9 %copy-done.1 = bf16[3,16,1536]{2,1,0:T(8,128)(2,1)S(1)} copy-done((bf16[3,16,1536]{2,1,0:T(8,128)(2,1)S(1)}, bf16[3,16,1536]{2,1,0:T(8,128)(2,1)}, u32[]{:S(2)}) %copy-start.1) | copy-done | bytes 147480
  3.5 0.0 copy-start.2
  3.5 0.7 %copy-done.2 = s32[12]{0:T(128)S(1)} copy-done((s32[12]{0:T(128)S(1)}, s32[12]{0:T(128)}, u32[]{:S(2)}) %copy-start.2) | copy-done | bytes 72
  4.1 52.2 %shard_map.59 = (bf16[128,1536]{1,0:T(8,128)(2,1)S(1)}, bf16[16,1536]{1,0:T(8,128)(2,1)S(1)}) custom-call(s32[12]{0:T(128)S(1)} %copy-done.2, s32[1]{0:T(128)S(6)} %copy.8.len_ref, bf16[3,128,1536]{2,1,0:T(8,128)(2,1)S(1)} %bitcast.2, bf16[3,16,1536]{2,1,0:T(8,128)(2,1)S(1)} %copy-done.1), custom_call_target="tpu_custom_call" | custom-call | tf_op jit(solution)/shard_map/pallas_call | solution.py:457
  56.4 0.7 %copy.9 = bf16[1,128,1536]{2,1,0:T(8,128)(2,1)} copy(bf16[1,128,1536]{2,1,0:T(8,128)(2,1)S(1)} %bitcast.3) | data formatting | bytes 786432
  57.1 0.6 %copy.10 = bf16[16,1536]{1,0:T(8,128)(2,1)} copy(bf16[16,1536]{1,0:T(8,128)(2,1)S(1)} %get-tuple-element.9) | data formatting | bytes 98304
Async XLA Ops:
  1.3 1.3 %copy-start = (bf16[3,1,128,1536]{3,2,1,0:T(8,128)(2,1)S(1)}, bf16[3,1,128,1536]{3,2,1,0:T(8,128)(2,1)}, u32[]{:S(2)}) copy-start(bf16[3,1,128,1536]{3,2,1,0:T(8,128)(2,1)} %param.4) | copy-start | bytes 3538948
  2.5 0.9 %copy-start.1 = (bf16[3,16,1536]{2,1,0:T(8,128)(2,1)S(1)}, bf16[3,16,1536]{2,1,0:T(8,128)(2,1)}, u32[]{:S(2)}) copy-start(bf16[3,16,1536]{2,1,0:T(8,128)(2,1)} %text_ref.1) | copy-start | bytes 442372
  3.5 0.7 %copy-start.2 = (s32[12]{0:T(128)S(1)}, s32[12]{0:T(128)}, u32[]{:S(2)}) copy-start(s32[12]{0:T(128)} %kind_ref.1) | copy-start | bytes 148

commit v2 on v1

--- a/solution.py
+++ b/solution.py
@@ -129,12 +129,16 @@
 def kernel(
     n,
     heads,
+    kind_hbm,
+    len_hbm,
+    video_hbm,
+    text_hbm,
+    video_out,
+    text_out,
     kind_ref,
     len_ref,
     video_ref,
     text_ref,
-    video_out,
-    text_out,
     pair_video,
     pair_text,
     q_all,
@@ -148,13 +152,16 @@
     m_send,
     m_recv,
     result,
+    in_sem,
     pair_s,
     pair_r,
     q_s,
+    qf_s,
     q_r,
     kv_s,
     kv_r,
     fw_s,
+    fy_s,
     t_s,
     t_r,
     o_s,
@@ -175,6 +182,8 @@
     scale = hd ** (-0.5)
     me = lax.axis_index("frame")
     parity = lax.rem(me, 2)
+    across = me + 2 - 4 * lax.rem(me // 2, 2)
+    row_count = n // 4
     partner = me + 1 - 2 * parity
     mine = me // 2
 
@@ -189,7 +198,22 @@
         )
         return c
 
+    inputs = [
+        pltpu.make_async_copy(a, b, in_sem.at[i])
+        for i, (a, b) in enumerate(
+            (
+                (kind_hbm, kind_ref),
+                (len_hbm, len_ref),
+                (text_hbm, text_ref),
+                (video_hbm, video_ref),
+            )
+        )
+    ]
+    for copy in inputs:
+        copy.start()
     lax.fori_loop(1, n, greet, 0)
+    for copy in inputs:
+        copy.wait()
 
     spatial_seen = jnp.int32(0)
     temporal_seen = jnp.int32(0)
@@ -223,8 +247,8 @@
 
     def pair_copies():
         return (
-            remote(video_ref.at[1:3], pair_video, pair_s.at[0], pair_r.at[0], partner),
-            remote(text_ref.at[1:3], pair_text, pair_s.at[1], pair_r.at[1], partner),
+            remote(video_hbm.at[1:3], pair_video, pair_s.at[0], pair_r.at[0], partner),
+            remote(text_hbm.at[1:3], pair_text, pair_s.at[1], pair_r.at[1], partner),
             remote(kv_all.at[me], kv_all.at[me], fw_s.at[mine], kv_r.at[me], partner),
         )
 
@@ -249,32 +273,56 @@
     def sent(src, sem):
         remote(src, src, sem, sem, partner).wait_send()
 
-    def start_q(k, c):
-        q_copy(twin(k)).start()
-        return c
-
-    def start_kv(k, c):
-        kv_copy(twin(k)).start()
-        return c
-
     def start_t(k, c):
         t_copy(lax.rem(me + k, n)).start()
         return c
 
-    lax.fori_loop(1, twins, start_q, 0)
+    def along(k):
+        return lax.rem(me + 4 * k, n)
+
+    def back(k):
+        return lax.rem(me + n - 4 * k, n)
+
+    def start_text(k, c):
+        q_copy(along(k)).start()
+        kv_copy(along(k)).start()
+        return c
+
+    q_copy(across).start()
+    lax.fori_loop(1, row_count, start_text, 0)
+    kv_copy(across).start()
     lax.fori_loop(1, n, start_t, 0)
-    lax.fori_loop(1, twins, start_kv, 0)
     t_recv[me] = t_send[me]
+
+    def qf_copy(j):
+        return remote(q_all.at[j // 2], q_all.at[j // 2], qf_s.at[j // 2], q_r.at[j // 2], across)
+
+    def fw_copy(j):
+        return remote(kv_all.at[j], kv_all.at[j], fw_s.at[j // 2], kv_r.at[j], partner)
+
+    def fy_copy(j):
+        return remote(kv_all.at[j], kv_all.at[j], fy_s.at[j // 2], kv_r.at[j], across)
+
+    def forward_text(k, c):
+        j = back(k)
+        landed(q_all.at[j // 2], q_r.at[j // 2])
+        qf_copy(j).start()
+        landed(kv_all.at[j], kv_r.at[j])
+        fy_copy(j).start()
+        fw_copy(j).start()
+        return c
+
+    lax.fori_loop(1, row_count, forward_text, 0)
 
     landed(pair_video, pair_r.at[0])
     landed(pair_text, pair_r.at[1])
 
     def wait_q(k, c):
-        j = twin(k) // 2
+        j = lax.rem(across + n - 4 * k, n) // 2
         landed(q_all.at[j], q_r.at[j])
         return c
 
-    lax.fori_loop(1, twins, wait_q, 0)
+    lax.fori_loop(0, row_count, wait_q, 0)
 
     length = len_ref[0]
     key = lax.broadcasted_iota(jnp.int32, (1, 2 * positions + 2 * shard), 1)
@@ -349,16 +397,13 @@
     lax.fori_loop(1, n, start_o, 0)
     o_recv[me] = o_send[me]
 
-    def fw_copy(j):
-        return remote(kv_all.at[j], kv_all.at[j], fw_s.at[j // 2], kv_r.at[j], partner)
-
     def forward(k, c):
-        j = lax.rem(me + n - 2 * k, n)
+        j = lax.rem(across + n - 4 * k, n)
         landed(kv_all.at[j], kv_r.at[j])
         fw_copy(j).start()
         return c
 
-    lax.fori_loop(1, twins, forward, 0)
+    lax.fori_loop(0, row_count, forward, 0)
 
     def wait_kv(k, c):
         j = lax.rem(partner + 2 * k, n)
@@ -424,10 +469,21 @@
     sent(pair_text, pair_s.at[1])
     sent(kv_all.at[me], fw_s.at[mine])
 
+    sent(q_all.at[mine], q_s.at[across // 2])
+    sent(kv_all.at[me], kv_s.at[across // 2])
+
+    def drain_row(k, c):
+        j = along(k) // 2
+        sent(q_all.at[j], q_s.at[j])
+        sent(kv_all.at[me], kv_s.at[j])
+        sent(q_all.at[j], qf_s.at[j])
+        sent(kv_all.at[me], fy_s.at[j])
+        return c
+
+    lax.fori_loop(1, row_count, drain_row, 0)
+
     def drain_twin(k, c):
         j = twin(k) // 2
-        sent(q_all.at[j], q_s.at[j])
-        sent(kv_all.at[me], kv_s.at[j])
         sent(kv_all.at[me], fw_s.at[j])
         sent(p_send.at[j], p_s.at[j])
         sent(m_send.at[j], m_s.at[j])
@@ -452,7 +508,7 @@
     hd = width // heads
     narrow = half * hd
     vmem = pl.BlockSpec(memory_space=pltpu.VMEM)
-    smem = pl.BlockSpec(memory_space=pltpu.SMEM)
+    hbm = pl.BlockSpec(memory_space=pltpu.HBM)
     dma = pltpu.SemaphoreType.DMA
     video_out, text_out = pl.pallas_call(
         functools.partial(kernel, n, heads),
@@ -460,9 +516,13 @@
             jax.ShapeDtypeStruct((positions, width), bf16),
             jax.ShapeDtypeStruct((shard, width), bf16),
         ),
-        in_specs=[smem, smem, vmem, vmem],
+        in_specs=[hbm] * 4,
         out_specs=(vmem, vmem),
         scratch_shapes=[
+            pltpu.SMEM((heads,), jnp.int32),
+            pltpu.SMEM((1,), jnp.int32),
+            pltpu.VMEM((3, positions, width), bf16),
+            pltpu.VMEM((3, shard, width), bf16),
             pltpu.VMEM((2, positions, width), bf16),
             pltpu.VMEM((2, shard, width), bf16),
             pltpu.VMEM((twins, shard, width), bf16),
@@ -476,12 +536,15 @@
             pltpu.VMEM((twins, shard, 128), f32),
             pltpu.VMEM((twins, shard, 128), f32),
             pltpu.VMEM((heads, positions, hd), bf16),
+            dma((4,)),
             dma((2,)),
             dma((2,)),
             dma((twins,)),
             dma((twins,)),
             dma((twins,)),
+            dma((twins,)),
             dma((n,)),
+            dma((twins,)),
             dma((twins,)),
             dma((n,)),
             dma((n,)),
@@ -493,7 +556,7 @@
             dma((twins,)),
         ],
         compiler_params=pltpu.CompilerParams(
-            collective_id=0, has_side_effects=True, vmem_limit_bytes=40 << 20
+            collective_id=0, has_side_effects=True, vmem_limit_bytes=63 << 20
         ),
     )(head_kind, text_len, video_qkv.reshape(3, positions, width), text_qkv)
     return video_out.reshape(1, positions, width), text_out
@@ -505,7 +568,7 @@
     shard = text_qkv.shape[1]
     whole_tiles = (
         video_qkv.shape[1] == 1
-        and n % 2 == 0
+        and n % 4 == 0
         and heads % 2 == 0
         and heads <= 64
         and shard % 16 == 0

time: 57.9 us -> 50 us (0.86)
  Pallas kernels: 52.2 us -> 45.2 us
  local copies, waits for them, and re-layouts: 4.2 us -> 3.19 us
    pallas_call x1, Pallas kernels: 52.2 us -> 45.2 us  [fused_body(): pl.pallas_call(functools.partial(kernel, n, heads), out_shape=(jax.ShapeD...]
    unnamed x8 -> x2, local copies, waits for them, and re-layouts: 4.2 us -> 3.19 us
where the time goes in v2:
time: 50 us; the launch traced here: 49.7 us
  Pallas kernels  45.2 us (90%)
  local copies, waits for them, and re-layouts  3.19 us (6%)
  between operations  1.29 us (3%)
    pallas_call x1, Pallas kernels, fused_body(): pl.pallas_call(functools.partial(kernel, n, heads), out_shape=(jax.ShapeD...  45.2 us
    unnamed x2, local copies, waits for them, and re-layouts  3.19 us

profile of v2, /device:TPU:0, one launch (start us, length us, event | category | flops | bytes accessed | tf_op | source)
XLA Modules:
  0.0 49.7 jit_solution(3181898962234725611)
XLA Ops:
  1.3 45.2 %shard_map.59 = (bf16[128,1536]{1,0:T(8,128)(2,1)}, bf16[16,1536]{1,0:T(8,128)(2,1)}) custom-call(s32[12]{0:T(128)} %kind_hbm.1, s32[1]{0:T(128)S(6)} %copy.8.len_hbm, bf16[3,128,1536]{2,1,0:T(8,128)(2,1)} %bitcast.2, bf16[3,16,1536]{2,1,0:T(8,128)(2,1)} %text_hbm.1), custom_call_target="tpu_custom_call" | custom-call | tf_op jit(solution)/shard_map/pallas_call | solution.py:513
  46.5 1.8 %copy.9 = bf16[1,128,1536]{2,1,0:T(8,128)(2,1)} copy(bf16[1,128,1536]{2,1,0:T(8,128)(2,1)} %bitcast.3) | data formatting | bytes 786432
  48.3 1.4 %copy.10 = bf16[16,1536]{1,0:T(8,128)(2,1)} copy(bf16[16,1536]{1,0:T(8,128)(2,1)} %get-tuple-element.9) | data formatting | bytes 98304

commit v3 on v2

--- a/solution.py
+++ b/solution.py
@@ -148,24 +148,29 @@
     o_send,
     o_recv,
     p_send,
+    p_mid,
+    p_out,
     p_recv,
     m_send,
+    m_mid,
+    m_out,
     m_recv,
     result,
     in_sem,
     pair_s,
     pair_r,
-    q_s,
-    qf_s,
+    up_s,
+    down_s,
+    side_s,
     q_r,
-    kv_s,
     kv_r,
     fw_s,
-    fy_s,
     t_s,
     t_r,
     o_s,
     o_r,
+    pa_s,
+    pa_r,
     p_s,
     p_r,
     m_s,
@@ -255,14 +260,8 @@
     for c in pair_copies():
         c.start()
 
-    def twin(k):
-        return lax.rem(me + 2 * k, n)
-
-    def q_copy(to):
-        return remote(q_all.at[mine], q_all.at[mine], q_s.at[to // 2], q_r.at[mine], to)
-
-    def kv_copy(to):
-        return remote(kv_all.at[me], kv_all.at[me], kv_s.at[to // 2], kv_r.at[me], to)
+    def along(k):
+        return lax.rem(me + 4 * k, n)
 
     def t_copy(to):
         return remote(t_send.at[to], t_recv.at[me], t_s.at[to], t_r.at[me], to)
@@ -277,42 +276,64 @@
         t_copy(lax.rem(me + k, n)).start()
         return c
 
-    def along(k):
-        return lax.rem(me + 4 * k, n)
-
-    def back(k):
-        return lax.rem(me + n - 4 * k, n)
-
-    def start_text(k, c):
-        q_copy(along(k)).start()
-        kv_copy(along(k)).start()
-        return c
-
-    q_copy(across).start()
-    lax.fori_loop(1, row_count, start_text, 0)
-    kv_copy(across).start()
+    row = me // 4
+    after, before = me + 4, me - 4
+
+    def hop(j, to, sems):
+        d = j // 2
+        return (
+            remote(q_all.at[d], q_all.at[d], sems.at[0, j // 4], q_r.at[d], to),
+            remote(kv_all.at[j], kv_all.at[j], sems.at[1, j // 4], kv_r.at[j], to),
+        )
+
+    def fw_copy(j):
+        return remote(kv_all.at[j], kv_all.at[j], fw_s.at[j // 2], kv_r.at[j], partner)
+
+    def hop_on(j, to, sems):
+        for copy in hop(j, to, sems):
+            copy.start()
+
+    @pl.when(row < row_count - 1)
+    def _():
+        hop_on(me, after, up_s)
+
+    @pl.when(row > 0)
+    def _():
+        hop_on(me, before, down_s)
+
+    hop_on(me, across, side_s)
     lax.fori_loop(1, n, start_t, 0)
     t_recv[me] = t_send[me]
 
-    def qf_copy(j):
-        return remote(q_all.at[j // 2], q_all.at[j // 2], qf_s.at[j // 2], q_r.at[j // 2], across)
-
-    def fw_copy(j):
-        return remote(kv_all.at[j], kv_all.at[j], fw_s.at[j // 2], kv_r.at[j], partner)
-
-    def fy_copy(j):
-        return remote(kv_all.at[j], kv_all.at[j], fy_s.at[j // 2], kv_r.at[j], across)
-
-    def forward_text(k, c):
-        j = back(k)
+    def arrive(j):
         landed(q_all.at[j // 2], q_r.at[j // 2])
-        qf_copy(j).start()
         landed(kv_all.at[j], kv_r.at[j])
-        fy_copy(j).start()
-        fw_copy(j).start()
-        return c
-
-    lax.fori_loop(1, row_count, forward_text, 0)
+
+    for k in range(1, row_count):
+
+        @pl.when(row >= k)
+        def _():
+            j = me - 4 * k
+            arrive(j)
+
+            @pl.when(row < row_count - 1)
+            def _():
+                hop_on(j, after, up_s)
+
+            hop_on(j, across, side_s)
+            fw_copy(j).start()
+
+        @pl.when(row + k < row_count)
+        def _():
+            j = me + 4 * k
+            arrive(j)
+
+            @pl.when(row > 0)
+            def _():
+                hop_on(j, before, down_s)
+
+            hop_on(j, across, side_s)
+            fw_copy(j).start()
 
     landed(pair_video, pair_r.at[0])
     landed(pair_text, pair_r.at[1])
@@ -344,28 +365,52 @@
         )
         s = jnp.where(key_ok, dot_nt(q, keys) * scale, masked_score)
         top, total, w = softmax_parts(s)
-        p_send[:, :, hs] = dot_nn(w, values).astype(bf16).reshape(twins, shard, hd)
+        part = dot_nn(w, values).astype(bf16).reshape(row_count, 2, shard, hd)
+        for y in range(2):
+            p_send[y, :, :, hs] = part[:, y]
         stats = jnp.where(lane == h, top, jnp.where(lane == h + 64, total, stats))
-    m_send[...] = stats.reshape(twins, shard, 128)
+    stats = stats.reshape(row_count, 2, shard, 128)
+    for y in range(2):
+        m_send[y] = stats[:, y]
+
+    column = lax.rem(mine, 2)
+    across_copies = (
+        remote(p_send.at[1 - column], p_mid, pa_s.at[0], pa_r.at[0], across),
+        remote(m_send.at[1 - column], m_mid, pa_s.at[1], pa_r.at[1], across),
+    )
+    for copy in across_copies:
+        copy.start()
+    landed(p_mid, pa_r.at[0])
+    landed(m_mid, pa_r.at[1])
+    for z in range(row_count):
+        ours, theirs = m_send[column, z], m_mid[z]
+        best = jnp.maximum(ours, theirs)
+        w_ours, w_theirs = jnp.exp(ours - best), jnp.exp(theirs - best)
+        total = pltpu.roll(w_ours, 64, 1) * ours + pltpu.roll(w_theirs, 64, 1) * theirs
+        m_out[z] = jnp.where(lax.broadcasted_iota(jnp.int32, best.shape, 1) < 64, best, total)
+        for h in range(heads):
+            hs = slice(h * hd, (h + 1) * hd)
+            p_out[z, :, hs] = (
+                w_ours[:, h : h + 1] * p_send[column, z, :, hs].astype(f32)
+                + w_theirs[:, h : h + 1] * p_mid[z, :, hs].astype(f32)
+            ).astype(bf16)
 
     def p_copy(to):
-        return remote(
-            p_send.at[to // 2], p_recv.at[mine], p_s.at[to // 2], p_r.at[mine], to
-        )
+        z = to // 4
+        return remote(p_out.at[z], p_recv.at[row], p_s.at[z], p_r.at[row], to)
 
     def m_copy(to):
-        return remote(
-            m_send.at[to // 2], m_recv.at[mine], m_s.at[to // 2], m_r.at[mine], to
-        )
+        z = to // 4
+        return remote(m_out.at[z], m_recv.at[row], m_s.at[z], m_r.at[row], to)
 
     def start_p(k, c):
-        p_copy(twin(k)).start()
-        m_copy(twin(k)).start()
-        return c
-
-    lax.fori_loop(1, twins, start_p, 0)
-    p_recv[mine] = p_send[mine]
-    m_recv[mine] = m_send[mine]
+        p_copy(along(k)).start()
+        m_copy(along(k)).start()
+        return c
+
+    lax.fori_loop(1, row_count, start_p, 0)
+    p_recv[row] = p_out[row]
+    m_recv[row] = m_out[row]
 
     def wait_t(k, c):
         j = lax.rem(me + k, n)
@@ -433,14 +478,14 @@
         video_out[:, h * hd : (h + 1) * hd] = block
 
     def wait_p(k, c):
-        j = twin(k) // 2
+        j = along(k) // 4
         landed(p_recv.at[j], p_r.at[j])
         landed(m_recv.at[j], m_r.at[j])
         return c
 
-    lax.fori_loop(1, twins, wait_p, 0)
+    lax.fori_loop(1, row_count, wait_p, 0)
     tops = m_recv[...]
-    sums = pltpu.roll(tops.reshape(rows, 128), 64, 1).reshape(twins, shard, 128)
+    sums = pltpu.roll(tops.reshape(row_count * shard, 128), 64, 1).reshape(tops.shape)
     best = tops.max(0, keepdims=True)
     weight = jnp.exp(jnp.minimum(tops - best, 0.0))
     total = (weight * sums).sum(0)
@@ -469,27 +514,39 @@
     sent(pair_text, pair_s.at[1])
     sent(kv_all.at[me], fw_s.at[mine])
 
-    sent(q_all.at[mine], q_s.at[across // 2])
-    sent(kv_all.at[me], kv_s.at[across // 2])
+    for copy in across_copies:
+        copy.wait_send()
+
+    def gone(sems, j):
+        sent(q_all.at[mine], sems.at[0, j])
+        sent(kv_all.at[me], sems.at[1, j])
+
+    for z in range(row_count):
+        gone(side_s, z)
+
+        @pl.when((z <= row) & (row < row_count - 1))
+        def _():
+            gone(up_s, z)
+
+        @pl.when((z >= row) & (row > 0))
+        def _():
+            gone(down_s, z)
 
     def drain_row(k, c):
-        j = along(k) // 2
-        sent(q_all.at[j], q_s.at[j])
-        sent(kv_all.at[me], kv_s.at[j])
-        sent(q_all.at[j], qf_s.at[j])
-        sent(kv_all.at[me], fy_s.at[j])
+        j = along(k)
+        sent(kv_all.at[me], fw_s.at[j // 2])
+        sent(p_out.at[0], p_s.at[j // 4])
+        sent(m_out.at[0], m_s.at[j // 4])
         return c
 
     lax.fori_loop(1, row_count, drain_row, 0)
 
-    def drain_twin(k, c):
-        j = twin(k) // 2
-        sent(kv_all.at[me], fw_s.at[j])
-        sent(p_send.at[j], p_s.at[j])
-        sent(m_send.at[j], m_s.at[j])
-        return c
-
-    lax.fori_loop(1, twins, drain_twin, 0)
+    def drain_across(k, c):
+        j = lax.rem(across + 4 * k, n)
+        sent(kv_all.at[me], fw_s.at[j // 2])
+        return c
+
+    lax.fori_loop(0, row_count, drain_across, 0)
 
     def drain_all(k, c):
         j = lax.rem(me + k, n)
@@ -507,6 +564,7 @@
     half, twins, piece = heads // 2, n // 2, positions // n
     hd = width // heads
     narrow = half * hd
+    rows = n // 4
     vmem = pl.BlockSpec(memory_space=pltpu.VMEM)
     hbm = pl.BlockSpec(memory_space=pltpu.HBM)
     dma = pltpu.SemaphoreType.DMA
@@ -531,29 +589,34 @@
             pltpu.VMEM((n, 3, piece, narrow), bf16),
             pltpu.VMEM((n, piece, narrow), bf16),
             pltpu.VMEM((n, piece, narrow), bf16),
-            pltpu.VMEM((twins, shard, width), bf16),
-            pltpu.VMEM((twins, shard, width), bf16),
-            pltpu.VMEM((twins, shard, 128), f32),
-            pltpu.VMEM((twins, shard, 128), f32),
+            pltpu.VMEM((2, rows, shard, width), bf16),
+            pltpu.VMEM((rows, shard, width), bf16),
+            pltpu.VMEM((rows, shard, width), bf16),
+            pltpu.VMEM((rows, shard, width), bf16),
+            pltpu.VMEM((2, rows, shard, 128), f32),
+            pltpu.VMEM((rows, shard, 128), f32),
+            pltpu.VMEM((rows, shard, 128), f32),
+            pltpu.VMEM((rows, shard, 128), f32),
             pltpu.VMEM((heads, positions, hd), bf16),
             dma((4,)),
             dma((2,)),
             dma((2,)),
-            dma((twins,)),
-            dma((twins,)),
-            dma((twins,)),
+            dma((2, rows)),
+            dma((2, rows)),
+            dma((2, rows)),
             dma((twins,)),
             dma((n,)),
-            dma((twins,)),
             dma((twins,)),
             dma((n,)),
             dma((n,)),
             dma((n,)),
             dma((n,)),
-            dma((twins,)),
-            dma((twins,)),
-            dma((twins,)),
-            dma((twins,)),
+            dma((2,)),
+            dma((2,)),
+            dma((rows,)),
+            dma((rows,)),
+            dma((rows,)),
+            dma((rows,)),
         ],
         compiler_params=pltpu.CompilerParams(
             collective_id=0, has_side_effects=True, vmem_limit_bytes=63 << 20

time: 50 us -> 53.3 us (1.066)
  Pallas kernels: 45.2 us -> 48.6 us
    pallas_call x1, Pallas kernels: 45.2 us -> 48.6 us  [fused_body(): pl.pallas_call(functools.partial(kernel, n, heads), out_shape=(jax.ShapeD...]
where the time goes in v3:
time: 53.3 us; the launch traced here: 53.1 us
  Pallas kernels  48.6 us (91%)
  local copies, waits for them, and re-layouts  3.19 us (6%)
  between operations  1.29 us (2%)
    pallas_call x1, Pallas kernels, fused_body(): pl.pallas_call(functools.partial(kernel, n, heads), out_shape=(jax.ShapeD...  48.6 us
    unnamed x2, local copies, waits for them, and re-layouts  3.19 us

profile of v3, /device:TPU:0, one launch (start us, length us, event | category | flops | bytes accessed | tf_op | source)
XLA Modules:
  0.0 53.1 jit_solution(12677872129248579143)
XLA Ops:
  1.3 48.6 %shard_map.59 = (bf16[128,1536]{1,0:T(8,128)(2,1)}, bf16[16,1536]{1,0:T(8,128)(2,1)}) custom-call(s32[12]{0:T(128)} %kind_hbm.1, s32[1]{0:T(128)S(6)} %copy.8.len_hbm, bf16[3,128,1536]{2,1,0:T(8,128)(2,1)} %bitcast.2, bf16[3,16,1536]{2,1,0:T(8,128)(2,1)} %text_hbm.1), custom_call_target="tpu_custom_call" | custom-call | tf_op jit(solution)/shard_map/pallas_call | solution.py:571
  49.9 1.8 %copy.9 = bf16[1,128,1536]{2,1,0:T(8,128)(2,1)} copy(bf16[1,128,1536]{2,1,0:T(8,128)(2,1)} %bitcast.3) | data formatting | bytes 786432
  51.7 1.4 %copy.10 = bf16[16,1536]{1,0:T(8,128)(2,1)} copy(bf16[16,1536]{1,0:T(8,128)(2,1)} %get-tuple-element.9) | data formatting | bytes 98304

commit v4 on v3

--- a/solution.py
+++ b/solution.py
@@ -302,8 +302,6 @@
         hop_on(me, before, down_s)
 
     hop_on(me, across, side_s)
-    lax.fori_loop(1, n, start_t, 0)
-    t_recv[me] = t_send[me]
 
     def arrive(j):
         landed(q_all.at[j // 2], q_r.at[j // 2])
@@ -335,6 +333,8 @@
             hop_on(j, across, side_s)
             fw_copy(j).start()
 
+    lax.fori_loop(1, n, start_t, 0)
+    t_recv[me] = t_send[me]
     landed(pair_video, pair_r.at[0])
     landed(pair_text, pair_r.at[1])
 
@@ -380,6 +380,36 @@
     )
     for copy in across_copies:
         copy.start()
+    def wait_t(k, c):
+        j = lax.rem(me + k, n)
+        landed(t_recv.at[j], t_r.at[j])
+        return c
+
+    lax.fori_loop(1, n, wait_t, 0)
+    count = n * piece
+    row_at = lax.rem(lax.broadcasted_iota(jnp.int32, (count, count), 0), piece)
+    col_at = lax.rem(lax.broadcasted_iota(jnp.int32, (count, count), 1), piece)
+    same = row_at == col_at
+    for i in range(half):
+        hs = slice(i * hd, (i + 1) * hd)
+        q, k_, v = (
+            t_recv[:, t, :, hs].astype(f32).reshape(count, hd).astype(bf16) for t in range(3)
+        )
+        s = jnp.where(same, dot_nt(q, k_) * scale, masked_score)
+        top, total, w = softmax_parts(s)
+        o = dot_nn(w, v) / total
+        o_send[:, :, hs] = o.reshape(n, piece, hd).astype(bf16)
+
+    def o_copy(to):
+        return remote(o_send.at[to], o_recv.at[me], o_s.at[to], o_r.at[me], to)
+
+    def start_o(k, c):
+        o_copy(lax.rem(me + k, n)).start()
+        return c
+
+    lax.fori_loop(1, n, start_o, 0)
+    o_recv[me] = o_send[me]
+
     landed(p_mid, pa_r.at[0])
     landed(m_mid, pa_r.at[1])
     for z in range(row_count):
@@ -411,36 +441,6 @@
     lax.fori_loop(1, row_count, start_p, 0)
     p_recv[row] = p_out[row]
     m_recv[row] = m_out[row]
-
-    def wait_t(k, c):
-        j = lax.rem(me + k, n)
-        landed(t_recv.at[j], t_r.at[j])
-        return c
-
-    lax.fori_loop(1, n, wait_t, 0)
-    count = n * piece
-    row_at = lax.rem(lax.broadcasted_iota(jnp.int32, (count, count), 0), piece)
-    col_at = lax.rem(lax.broadcasted_iota(jnp.int32, (count, count), 1), piece)
-    same = row_at == col_at
-    for i in range(half):
-        hs = slice(i * hd, (i + 1) * hd)
-        q, k_, v = (
-            t_recv[:, t, :, hs].astype(f32).reshape(count, hd).astype(bf16) for t in range(3)
-        )
-        s = jnp.where(same, dot_nt(q, k_) * scale, masked_score)
-        top, total, w = softmax_parts(s)
-        o = dot_nn(w, v) / total
-        o_send[:, :, hs] = o.reshape(n, piece, hd).astype(bf16)
-
-    def o_copy(to):
-        return remote(o_send.at[to], o_recv.at[me], o_s.at[to], o_r.at[me], to)
-
-    def start_o(k, c):
-        o_copy(lax.rem(me + k, n)).start()
-        return c
-
-    lax.fori_loop(1, n, start_o, 0)
-    o_recv[me] = o_send[me]
 
     def forward(k, c):
         j = lax.rem(across + n - 4 * k, n)

time: 53.3 us -> 48.1 us (0.902)
  Pallas kernels: 48.6 us -> 43.4 us
    pallas_call x1, Pallas kernels: 48.6 us -> 43.4 us  [fused_body(): pl.pallas_call(functools.partial(kernel, n, heads), out_shape=(jax.ShapeD...]
where the time goes in v4:
time: 48.1 us; the launch traced here: 47.8 us
  Pallas kernels  43.4 us (90%)
  local copies, waits for them, and re-layouts  3.19 us (7%)
  between operations  1.29 us (3%)
    pallas_call x1, Pallas kernels, fused_body(): pl.pallas_call(functools.partial(kernel, n, heads), out_shape=(jax.ShapeD...  43.4 us
    unnamed x2, local copies, waits for them, and re-layouts  3.19 us

profile of v4, /device:TPU:0, one launch (start us, length us, event | category | flops | bytes accessed | tf_op | source)
XLA Modules:
  0.0 47.8 jit_solution(6360411681337346608)
XLA Ops:
  1.3 43.4 %shard_map.59 = (bf16[128,1536]{1,0:T(8,128)(2,1)}, bf16[16,1536]{1,0:T(8,128)(2,1)}) custom-call(s32[12]{0:T(128)} %kind_hbm.1, s32[1]{0:T(128)S(6)} %copy.8.len_hbm, bf16[3,128,1536]{2,1,0:T(8,128)(2,1)} %bitcast.2, bf16[3,16,1536]{2,1,0:T(8,128)(2,1)} %text_hbm.1), custom_call_target="tpu_custom_call" | custom-call | tf_op jit(solution)/shard_map/pallas_call | solution.py:571
  44.6 1.8 %copy.9 = bf16[1,128,1536]{2,1,0:T(8,128)(2,1)} copy(bf16[1,128,1536]{2,1,0:T(8,128)(2,1)} %bitcast.3) | data formatting | bytes 786432
  46.4 1.4 %copy.10 = bf16[16,1536]{1,0:T(8,128)(2,1)} copy(bf16[16,1536]{1,0:T(8,128)(2,1)} %get-tuple-element.9) | data formatting | bytes 98304

commit v5 on v4

--- a/solution.py
+++ b/solution.py
@@ -217,7 +217,7 @@
     for copy in inputs:
         copy.start()
     lax.fori_loop(1, n, greet, 0)
-    for copy in inputs:
+    for copy in inputs[:3]:
         copy.wait()
 
     spatial_seen = jnp.int32(0)
@@ -242,96 +242,97 @@
             kv_all[me, t, :, i * hd : (i + 1) * hd] = in_slot(i, lambda c: text_ref[t + 1, :, c])
     q_all[mine] = text_ref[0]
 
+    pl.semaphore_wait(barrier, n - 1)
+
+    def pair_copies():
+        return (
+            remote(video_hbm.at[1:3], pair_video, pair_s.at[0], pair_r.at[0], partner),
+            remote(text_hbm.at[1:3], pair_text, pair_s.at[1], pair_r.at[1], partner),
+            remote(kv_all.at[me], kv_all.at[me], fw_s.at[mine], kv_r.at[me], partner),
+        )
+
+    for c in pair_copies():
+        c.start()
+
+    def along(k):
+        return lax.rem(me + 4 * k, n)
+
+    def t_copy(to):
+        return remote(t_send.at[to], t_recv.at[me], t_s.at[to], t_r.at[me], to)
+
+    def landed(dst, sem):
+        remote(dst, dst, sem, sem, partner).wait_recv()
+
+    def sent(src, sem):
+        remote(src, src, sem, sem, partner).wait_send()
+
+    def start_t(k, c):
+        t_copy(lax.rem(me + k, n)).start()
+        return c
+
+    row = me // 4
+    after, before = me + 4, me - 4
+
+    def hop(j, to, sems):
+        d = j // 2
+        return (
+            remote(q_all.at[d], q_all.at[d], sems.at[0, j // 4], q_r.at[d], to),
+            remote(kv_all.at[j], kv_all.at[j], sems.at[1, j // 4], kv_r.at[j], to),
+        )
+
+    def fw_copy(j):
+        return remote(kv_all.at[j], kv_all.at[j], fw_s.at[j // 2], kv_r.at[j], partner)
+
+    def hop_on(j, to, sems):
+        for copy in hop(j, to, sems):
+            copy.start()
+
+    @pl.when(row < row_count - 1)
+    def _():
+        hop_on(me, after, up_s)
+
+    @pl.when(row > 0)
+    def _():
+        hop_on(me, before, down_s)
+
+    hop_on(me, across, side_s)
+
+    def arrive(j):
+        landed(q_all.at[j // 2], q_r.at[j // 2])
+        landed(kv_all.at[j], kv_r.at[j])
+
+    for k in range(1, row_count):
+
+        @pl.when(row >= k)
+        def _():
+            j = me - 4 * k
+            arrive(j)
+
+            @pl.when(row < row_count - 1)
+            def _():
+                hop_on(j, after, up_s)
+
+            hop_on(j, across, side_s)
+            fw_copy(j).start()
+
+        @pl.when(row + k < row_count)
+        def _():
+            j = me + 4 * k
+            arrive(j)
+
+            @pl.when(row > 0)
+            def _():
+                hop_on(j, before, down_s)
+
+            hop_on(j, across, side_s)
+            fw_copy(j).start()
+
+    inputs[3].wait()
     for i in range(half):
         for t in range(3):
             whole = in_slot(half + i, lambda c: video_ref[t, :, c])
             whole = whole.astype(f32).reshape(n, piece, hd)
             t_send[:, t, :, i * hd : (i + 1) * hd] = whole.astype(bf16)
-
-    pl.semaphore_wait(barrier, n - 1)
-
-    def pair_copies():
-        return (
-            remote(video_hbm.at[1:3], pair_video, pair_s.at[0], pair_r.at[0], partner),
-            remote(text_hbm.at[1:3], pair_text, pair_s.at[1], pair_r.at[1], partner),
-            remote(kv_all.at[me], kv_all.at[me], fw_s.at[mine], kv_r.at[me], partner),
-        )
-
-    for c in pair_copies():
-        c.start()
-
-    def along(k):
-        return lax.rem(me + 4 * k, n)
-
-    def t_copy(to):
-        return remote(t_send.at[to], t_recv.at[me], t_s.at[to], t_r.at[me], to)
-
-    def landed(dst, sem):
-        remote(dst, dst, sem, sem, partner).wait_recv()
-
-    def sent(src, sem):
-        remote(src, src, sem, sem, partner).wait_send()
-
-    def start_t(k, c):
-        t_copy(lax.rem(me + k, n)).start()
-        return c
-
-    row = me // 4
-    after, before = me + 4, me - 4
-
-    def hop(j, to, sems):
-        d = j // 2
-        return (
-            remote(q_all.at[d], q_all.at[d], sems.at[0, j // 4], q_r.at[d], to),
-            remote(kv_all.at[j], kv_all.at[j], sems.at[1, j // 4], kv_r.at[j], to),
-        )
-
-    def fw_copy(j):
-        return remote(kv_all.at[j], kv_all.at[j], fw_s.at[j // 2], kv_r.at[j], partner)
-
-    def hop_on(j, to, sems):
-        for copy in hop(j, to, sems):
-            copy.start()
-
-    @pl.when(row < row_count - 1)
-    def _():
-        hop_on(me, after, up_s)
-
-    @pl.when(row > 0)
-    def _():
-        hop_on(me, before, down_s)
-
-    hop_on(me, across, side_s)
-
-    def arrive(j):
-        landed(q_all.at[j // 2], q_r.at[j // 2])
-        landed(kv_all.at[j], kv_r.at[j])
-
-    for k in range(1, row_count):
-
-        @pl.when(row >= k)
-        def _():
-            j = me - 4 * k
-            arrive(j)
-
-            @pl.when(row < row_count - 1)
-            def _():
-                hop_on(j, after, up_s)
-
-            hop_on(j, across, side_s)
-            fw_copy(j).start()
-
-        @pl.when(row + k < row_count)
-        def _():
-            j = me + 4 * k
-            arrive(j)
-
-            @pl.when(row > 0)
-            def _():
-                hop_on(j, before, down_s)
-
-            hop_on(j, across, side_s)
-            fw_copy(j).start()
 
     lax.fori_loop(1, n, start_t, 0)
     t_recv[me] = t_send[me]

time: 48.1 us -> 47.7 us (level)
  Pallas kernels: 43.4 us -> 42.9 us
where the time goes in v5:
time: 47.7 us; the launch traced here: 47.4 us
  Pallas kernels  42.9 us (90%)
  local copies, waits for them, and re-layouts  3.19 us (7%)
  between operations  1.29 us (3%)
    pallas_call x1, Pallas kernels, fused_body(): pl.pallas_call(functools.partial(kernel, n, heads), out_shape=(jax.ShapeD...  42.9 us
    unnamed x2, local copies, waits for them, and re-layouts  3.19 us

profile of v5, /device:TPU:0, one launch (start us, length us, event | category | flops | bytes accessed | tf_op | source)
XLA Modules:
  0.0 47.4 jit_solution(5236622964007635342)
XLA Ops:
  1.3 42.9 %shard_map.59 = (bf16[128,1536]{1,0:T(8,128)(2,1)}, bf16[16,1536]{1,0:T(8,128)(2,1)}) custom-call(s32[12]{0:T(128)} %kind_hbm.1, s32[1]{0:T(128)S(6)} %copy.8.len_hbm, bf16[3,128,1536]{2,1,0:T(8,128)(2,1)} %bitcast.2, bf16[3,16,1536]{2,1,0:T(8,128)(2,1)} %text_hbm.1), custom_call_target="tpu_custom_call" | custom-call | tf_op jit(solution)/shard_map/pallas_call | solution.py:572
  44.2 1.8 %copy.9 = bf16[1,128,1536]{2,1,0:T(8,128)(2,1)} copy(bf16[1,128,1536]{2,1,0:T(8,128)(2,1)} %bitcast.3) | data formatting | bytes 786432
  46.0 1.4 %copy.10 = bf16[16,1536]{1,0:T(8,128)(2,1)} copy(bf16[16,1536]{1,0:T(8,128)(2,1)} %get-tuple-element.9) | data formatting | bytes 98304

commit v6 on v5

--- a/solution.py
+++ b/solution.py
@@ -334,7 +334,8 @@
             whole = whole.astype(f32).reshape(n, piece, hd)
             t_send[:, t, :, i * hd : (i + 1) * hd] = whole.astype(bf16)
 
-    lax.fori_loop(1, n, start_t, 0)
+    lax.fori_loop(twins, n, start_t, 0)
+    lax.fori_loop(1, twins, start_t, 0)
     t_recv[me] = t_send[me]
     landed(pair_video, pair_r.at[0])
     landed(pair_text, pair_r.at[1])

time: 47.7 us -> 48.2 us (1.010)
  Pallas kernels: 42.9 us -> 43.5 us
    pallas_call x1, Pallas kernels: 42.9 us -> 43.5 us  [fused_body(): pl.pallas_call(functools.partial(kernel, n, heads), out_shape=(jax.ShapeD...]
where the time goes in v6:
time: 48.2 us; the launch traced here: 48 us
  Pallas kernels  43.5 us (90%)
  local copies, waits for them, and re-layouts  3.19 us (7%)
  between operations  1.29 us (3%)
    pallas_call x1, Pallas kernels, fused_body(): pl.pallas_call(functools.partial(kernel, n, heads), out_shape=(jax.ShapeD...  43.5 us
    unnamed x2, local copies, waits for them, and re-layouts  3.19 us

profile of v6, /device:TPU:0, one launch (start us, length us, event | category | flops | bytes accessed | tf_op | source)
XLA Modules:
  0.0 48.0 jit_solution(16690880963573591640)
XLA Ops:
  1.3 43.5 %shard_map.59 = (bf16[128,1536]{1,0:T(8,128)(2,1)}, bf16[16,1536]{1,0:T(8,128)(2,1)}) custom-call(s32[12]{0:T(128)} %kind_hbm.1, s32[1]{0:T(128)S(6)} %copy.8.len_hbm, bf16[3,128,1536]{2,1,0:T(8,128)(2,1)} %bitcast.2, bf16[3,16,1536]{2,1,0:T(8,128)(2,1)} %text_hbm.1), custom_call_target="tpu_custom_call" | custom-call | tf_op jit(solution)/shard_map/pallas_call | solution.py:573
  44.8 1.8 %copy.9 = bf16[1,128,1536]{2,1,0:T(8,128)(2,1)} copy(bf16[1,128,1536]{2,1,0:T(8,128)(2,1)} %bitcast.3) | data formatting | bytes 786432
  46.6 1.4 %copy.10 = bf16[16,1536]{1,0:T(8,128)(2,1)} copy(bf16[16,1536]{1,0:T(8,128)(2,1)} %get-tuple-element.9) | data formatting | bytes 98304
